TPU v7x, 256 devices: a whole 4x4x8 slice. The times are simulated.
256 devices in a mesh: tm: 8 (over z_lo, y), space: 32 (over z_hi, x, core).
Axes of the slice: x: 4, y: 4, z: 8 (z_hi: 4, z_lo: 2; z = z_hi * 2 + z_lo), core: 2. Of those that a mesh axis runs over, the one named last changes fastest.
Arguments:
- control: float32 [256, 51200], P(('tm', 'space')), may hold values from -4 to 4
- spectrum: float32 [51200], replicated, may hold values from 0.2 to 2
- perturb: bfloat16 [16, 256, 4, 51200], P('tm', None, None, 'space'), may hold values from -0.375 to 0.375
- obs_index: int32 [16, 65536], P('tm', 'space'), may hold values from 0 to 6399
- innovation: float32 [16, 65536], P('tm', 'space'), may hold values from -10 to 10
- obs_sigma: float32 [16, 65536], P('tm', 'space'), may hold values from 0.5 to 2
- qc_class: int32 [16, 65536], P('tm', 'space'), may hold values from 0 to 2
Outputs:
- control_out: float32 [256, 51200], P(('tm', 'space'))
- cost_list: float32 [1], replicated
Inputs may be any that keep to these rules, and one draw needn't show every extreme that they name: `obs_index`: observation o of block o // 2048 observes the cell level * 1600 + point, the point counted within the block's piece of the grid; repeats may occur.
All inputs are finite; a program needn't handle non-finite values.
Results may differ from a plain program's by a relative error of at most 0.0034.
Values may be sent and summed in bfloat16 or wider, within the bound.
No kernel may reach another device: no remote copies, remote signals or barrier semaphores. Data moves between devices by JAX's collectives and lax.ppermute only.
A program may use at most 128 MiB of HBM per device.

v0:
```python
import jax
import jax.numpy as jnp
from jax import lax
from jax.sharding import Mesh
from jax.sharding import PartitionSpec as P

GX = 320
GY = 160
SPACE = ("space_0", "space_1", "space_2")
TM = ("tm_0", "tm_1")
TM_SPACE = ("tm_0", "tm_1", "space_0", "space_1", "space_2")


def joined_along(tiles, dim):
    lengths = list(tiles.shape[1:])
    lengths[dim] *= tiles.shape[0]
    return jnp.moveaxis(tiles, 0, dim).reshape(lengths)


def from_everyone(value, axis):
    copies = jnp.broadcast_to(value, (lax.axis_size(axis), *value.shape))
    return lax.all_to_all(copies, axis, split_axis=0, concat_axis=0, tiled=True)


def gather_directly(value, axis, dim):
    return joined_along(from_everyone(value, axis), dim)


def cut_along(value, dim, count):
    lengths = value.shape
    tiles = value.reshape(*lengths[:dim], count, lengths[dim] // count, *lengths[dim + 1 :])
    return jnp.moveaxis(tiles, dim, 0)


def sent_and_summed(value, axis, dim):
    tiles = cut_along(value, dim, lax.axis_size(axis))
    arrived = lax.all_to_all(tiles, axis, split_axis=0, concat_axis=0, tiled=True)
    return arrived.astype(jnp.float32).sum(axis=0)


def by_axis(value, axes):
    for axis in axes:
        value = lax.psum(value, axis)
    return value


def lookup_tables(segment_length):
    wave_num = jnp.arange(segment_length, dtype=jnp.float32)[:, None]
    grid_positions = jnp.arange(segment_length, dtype=jnp.float32)[None, :]
    basis = jnp.cos(jnp.pi * (grid_positions + 0.5) * wave_num / segment_length) * jnp.sqrt(
        2.0 / segment_length
    )
    return jnp.where(wave_num == 0, basis * jnp.sqrt(0.5), basis)


def synthesize(control, spectrum, basis_x, basis_y):
    coeffs = (control * spectrum[None, :]).reshape(control.shape[0], GX, GY)
    middle = jnp.einsum("kn,mkl->mnl", basis_x, coeffs, precision=lax.Precision.HIGHEST)
    result = jnp.einsum("mnl,lp->mnp", middle, basis_y, precision=lax.Precision.HIGHEST)
    return result.reshape(control.shape[0], GX * GY)


def analyze(adjoint, spectrum, basis_x, basis_y):
    state_fields = adjoint.reshape(adjoint.shape[0], GX, GY)
    middle = jnp.einsum("kn,mnp->mkp", basis_x, state_fields, precision=lax.Precision.HIGHEST)
    result = jnp.einsum("mkp,lp->mkl", middle, basis_y, precision=lax.Precision.HIGHEST)
    return result.reshape(adjoint.shape[0], GX * GY) * spectrum[None, :]


def per_device(control, spectrum, perturb, obs_index, innovation, obs_sigma, qc_class):
    basis_x = lookup_tables(GX)
    basis_y = lookup_tables(GY)
    slot_count = perturb.shape[0]
    levels = perturb.shape[2]
    piece_len = perturb.shape[3]
    radius = jnp.where(qc_class == 0, 4.0, jnp.where(qc_class == 1, 2.0, 1.0)).astype(jnp.float32)

    def scatter_cells(indices, values):
        return jnp.zeros((levels * piece_len,), jnp.float32).at[indices].add(values)

    member_field = synthesize(control, spectrum, basis_x, basis_y).astype(jnp.bfloat16)
    pieces = lax.all_to_all(member_field, SPACE, split_axis=1, concat_axis=0, tiled=True)
    selected_entries = perturb
    increment = jnp.einsum(
        "dzab,zb->dab",
        selected_entries,
        gather_directly(pieces, TM, 0),
        preferred_element_type=jnp.float32,
    )
    cells_flat = increment.reshape(slot_count, levels * piece_len)
    modelled = jnp.take_along_axis(cells_flat, obs_index, axis=1)
    scaled = (modelled - innovation) / obs_sigma
    scaled_sq = scaled * scaled / (radius * radius)
    obs_part = jnp.sum(0.5 * radius * radius * jnp.log1p(scaled_sq))
    back_part = 0.5 * jnp.sum(control * control)
    obs_grad = scaled / ((1.0 + scaled_sq) * obs_sigma)
    control_update = jax.vmap(scatter_cells)(obs_index, obs_grad).astype(jnp.bfloat16)
    control_update = control_update.reshape(slot_count, levels, piece_len)
    selected_entries = perturb
    summed_rows = sent_and_summed(
        jnp.einsum(
            "qiyr,qyr->ir", selected_entries, control_update, preferred_element_type=jnp.float32
        ).astype(jnp.bfloat16),
        TM,
        0,
    )
    adjoint = lax.all_to_all(
        summed_rows.astype(jnp.bfloat16), SPACE, split_axis=0, concat_axis=1, tiled=True
    ).astype(summed_rows.dtype)
    gradient = control + analyze(adjoint, spectrum, basis_x, basis_y)
    grad_part = jnp.sum(gradient * gradient)
    obs_cost = by_axis(obs_part, TM_SPACE)
    back_cost = by_axis(back_part, TM_SPACE)
    grad_sq = by_axis(grad_part, TM_SPACE)
    total_cost = back_cost + obs_cost
    step_size = 0.5 * total_cost / (grad_sq + 1e-06)
    control = control - step_size * gradient
    cost_list = [total_cost]
    return (control, jnp.stack(cost_list))


def solution(mesh):
    split = Mesh(
        mesh.devices.reshape(2, 4, 4, 4, 2), ("tm_0", "tm_1", "space_0", "space_1", "space_2")
    )
    return jax.shard_map(
        per_device,
        mesh=split,
        in_specs=(
            P(TM_SPACE, None),
            P(),
            P(TM, None, None, SPACE),
            P(TM, SPACE),
            P(TM, SPACE),
            P(TM, SPACE),
            P(TM, SPACE),
        ),
        out_specs=(P(TM_SPACE, None), P()),
        check_vma=False,
    )
```

profile of v0, /device:TPU:1, one launch (start us, length us, event | category | flops | bytes accessed | tf_op | source)
XLA Modules:
  0.0 200.4 jit_solution(14478216009850965294)
XLA Ops:
  0.7 2.4 %multiply_reduce_fusion.4 = (f32[]{:T(128)}, f32[51200]{0:T(1024)S(1)}) fusion(f32[1,51200]{1,0:T(1,128)} %param.7, f32[1,51200]{1,0:T(1,128)} %bitcast.57), kind=kLoop, calls=%fused_computation.22 | loop fusion | flops 153599 | bytes 614404 | tf_op jit(solution)/shard_map/reduce_sum | solution.py:95
  3.2 2.6 %convolution_bitcast_fusion.1 = f32[320,160]{0,1:T(8,128)S(1)} fusion(f32[320,160]{1,0:T(8,128)S(1)} %reshape.104, f32[320]{0:T(512)S(1)} %add_multiply_fusion, pred[320]{0:T(512)(128)(4,1)S(1)} %iota_compare_fusion), kind=kOutput, calls=%fused_computation.5 | convolution fusion | flops 197120000 | bytes 411200 | tf_op jit(solution)/shard_map/kn,mkl->mnl/dot_general | solution.py:58
  5.8 1.1 convolution_convert_fusion
  7.0 0.3 convert_element_type.33
  7.3 0.5 broadcast.94
  7.9 1.3 reduce.14
  9.3 23.1 %all_to_all.36 = bf16[32,2,800]{2,1,0:T(2,128)(2,1)S(1)} all-to-all(bf16[32,2,800]{2,1,0:T(2,128)(2,1)S(1)} %reshape.146), channel_id=1, replica_groups=mesh['tm_0'=2,'tm_1'=4,'space_0'=4,'space_1'=4,'space_2'=2] {'space_0','..., dimensions={0} | all-to-all | bytes 204800 | tf_op jit(solution)/shard_map/all_to_all | solution.py:82
  32.7 1.0 broadcast_in_dim.57
  33.6 4.5 %all-to-all-start.1 = ((bf16[8,32,1600]{2,1,0:T(8,128)(2,1)}), bf16[8,32,1600]{2,1,0:T(8,128)(2,1)S(1)}, u32[]{:S(2)}, u32[]{:S(2)}) async-start(bf16[8,32,1600]{2,1,0:T(8,128)(2,1)} %broadcast_in_dim.57), calls=%async_computation.1 | async-start | bytes 1703936 | tf_op jit(solution)/shard_map/all_to_all | solution.py:22
  38.5 12.5 %all-to-all-done.1 = bf16[8,32,1600]{2,1,0:T(8,128)(2,1)S(1)} async-done(((bf16[8,32,1600]{2,1,0:T(8,128)(2,1)}), bf16[8,32,1600]{2,1,0:T(8,128)(2,1)S(1)}, u32[]{:S(2)}, u32[]{:S(2)}) %all-to-all-start.1) | async-done | bytes 819232 | tf_op jit(solution)/shard_map/all_to_all | solution.py:22
  51.1 0.7 copy.34
  51.9 4.7 %multiply_reduce_fusion.1 = f32[1600,2,4]{0,2,1:T(4,128)S(1)} fusion(f32[1600,256]{1,0:T(8,128)S(1)} %copy.34, bf16[2,256,4,1600]{1,3,2,0:T(8,128)(2,1)} %param.9), kind=kLoop, calls=%fused_computation.3 | loop fusion | flops 9817600 | bytes 8243200 | tf_op jit(solution)/shard_map/dzab,zb->dab/dot_general | solution.py:84
  56.7 34.9 %gather_fusion = f32[4096]{0:T(1024)S(1)} fusion(f32[2,6400]{1,0:T(2,128)S(1)} %reshape.107, s32[4096]{0:T(1024)S(1)} %bitcast.53), kind=kCustom, calls=%fused_computation | custom fusion | bytes 65536 | tf_op jit(solution)/shard_map/jit(take_along_axis)/gather | solution.py:91
  91.7 0.8 fusion.26
  92.5 22.1 %scatter_custom_fusion = f32[12800]{0:T(1024)S(1)} fusion(s32[4096]{0:T(1024)S(1)} %bitcast.62, f32[4096]{0:T(1024)S(1)} %bitcast.63, f32[]{:T(128)} %constant.18.clone.1), kind=kCustom, calls=%fused_computation.44 | custom fusion | flops 4096 | bytes 51204
  114.7 4.8 %multiply_reduce_fusion = bf16[1600,256]{1,0:T(8,128)(2,1)S(1)} fusion(f32[1600,2,4]{0,2,1:T(4,128)S(1)} %bitcast_convert_fusion.1, bf16[2,256,4,1600]{1,3,2,0:T(8,128)(2,1)} %param.9), kind=kLoop, calls=%fused_computation.2 | loop fusion | flops 9420800 | bytes 7424000
  119.5 0.7 copy.31
  120.2 16.1 %all_to_all.37 = bf16[8,32,1600]{2,1,0:T(8,128)(2,1)S(1)} all-to-all(bf16[8,32,1600]{2,1,0:T(8,128)(2,1)S(1)} %bitcast.54), channel_id=1, replica_groups=mesh['tm_0'=2,'tm_1'=4,'space_0'=4,'space_1'=4,'space_2'=2] {'tm_0','tm_1'}, dimensions={0} | all-to-all | bytes 1638400 | tf_op jit(solution)/shard_map/all_to_all | solution.py:37
  136.5 0.7 reduce.15
  137.2 0.8 reshape.148
  138.0 5.6 %all-to-all-start.3 = ((bf16[32,2,800]{2,1,0:T(2,128)(2,1)}), bf16[32,2,800]{2,1,0:T(2,128)(2,1)S(1)}, u32[]{:S(2)}, u32[]{:S(2)}) async-start(bf16[32,2,800]{2,1,0:T(2,128)(2,1)} %reshape.148), calls=%async_computation.3 | async-start | bytes 229376 | tf_op jit(solution)/shard_map/all_to_all | solution.py:107
  145.0 9.2 %all-to-all-done.3 = bf16[32,2,800]{2,1,0:T(2,128)(2,1)S(1)} async-done(((bf16[32,2,800]{2,1,0:T(2,128)(2,1)}), bf16[32,2,800]{2,1,0:T(2,128)(2,1)S(1)}, u32[]{:S(2)}, u32[]{:S(2)}) %all-to-all-start.3) | async-done | bytes 102432 | tf_op jit(solution)/shard_map/all_to_all | solution.py:107
  154.4 0.7 reduce.6
  155.3 2.3 %convolution_bitcast_fusion = f32[320,160]{0,1:T(8,128)S(1)} fusion(bf16[320,160]{1,0:T(8,128)(2,1)S(1)} %reshape.111, f32[320]{0:T(512)S(1)} %add_multiply_fusion, pred[320]{0:T(512)(128)(4,1)S(1)} %iota_compare_fusion), kind=kOutput, calls=%fused_computation.4 | convolution fusion | flops 197120000 | bytes 308800 | tf_op jit(solution)/shard_map/kn,mnp->mkp/dot_general | solution.py:65
  157.6 1.3 fusion.10
  159.2 1.0 multiply_reduce_fusion.2
  160.3 4.4 %all-reduce.4 = (f32[]{:T(128)}, f32[]{:T(128)}) all-reduce(f32[]{:T(128)S(6)} %add.87, f32[]{:T(128)} %get-tuple-element.14), channel_id=1, replica_groups=mesh['tm_0'=2,'tm_1'=4,'space_0'=4,'space_1'=4,'space_2'=2] {'tm_0'}, use_global_device_ids=true, to_apply=%region_1.2 | all-reduce | flops 2 | bytes 16 | tf_op jit(solution)/shard_map/psum | solution.py:43
  164.7 7.7 %all-reduce.2 = (f32[]{:T(128)}, f32[]{:T(128)}) all-reduce(f32[]{:T(128)} %get-tuple-element.12, f32[]{:T(128)} %get-tuple-element.13), channel_id=1, replica_groups=mesh['tm_0'=2,'tm_1'=4,'space_0'=4,'space_1'=4,'space_2'=2] {'tm_1'}, use_global_device_ids=true, to_apply=%region_2.3 | all-reduce | flops 2 | bytes 16 | tf_op jit(solution)/shard_map/psum | solution.py:43
  172.4 8.3 %all-reduce.1 = (f32[]{:T(128)}, f32[]{:T(128)}) all-reduce(f32[]{:T(128)} %get-tuple-element.8, f32[]{:T(128)} %get-tuple-element.9), channel_id=1, replica_groups=mesh['tm_0'=2,'tm_1'=4,'space_0'=4,'space_1'=4,'space_2'=2] {'space_0'}, use_global_device_ids=true, to_apply=%region_3.4 | all-reduce | flops 2 | bytes 16 | tf_op jit(solution)/shard_map/psum | solution.py:43
  180.7 7.0 %all-reduce = (f32[]{:T(128)}, f32[]{:T(128)}) all-reduce(f32[]{:T(128)} %get-tuple-element.6, f32[]{:T(128)} %get-tuple-element.7), channel_id=1, replica_groups=mesh['tm_0'=2,'tm_1'=4,'space_0'=4,'space_1'=4,'space_2'=2] {'space_1'}, use_global_device_ids=true, to_apply=%region_4.5 | all-reduce | flops 2 | bytes 16 | tf_op jit(solution)/shard_map/psum | solution.py:43
  187.7 10.6 %all-reduce.3 = (f32[]{:T(128)}, f32[]{:T(128)}) all-reduce(f32[]{:T(128)} %get-tuple-element.4, f32[]{:T(128)} %get-tuple-element.5), channel_id=1, replica_groups=mesh['tm_0'=2,'tm_1'=4,'space_0'=4,'space_1'=4,'space_2'=2] {'space_2'}, use_global_device_ids=true, to_apply=%region_5.6 | all-reduce | flops 2 | bytes 16 | tf_op jit(solution)/shard_map/psum | solution.py:43
  199.5 0.9 multiply_subtract_fusion
  (46 shorter events, 2.2 us)
Async XLA Ops:
  7.3 30.8 %copy-start.2 = (s32[2,2048]{1,0:T(2,128)S(1)}, s32[2,2048]{1,0:T(2,128)}, u32[]{:S(2)}) copy-start(s32[2,2048]{1,0:T(2,128)} %param.10) | copy-start | bytes 49156
  7.9 30.4 %copy-start.6 = (s32[2]{0:T(128)S(1)}, s32[2]{0:T(128)}, u32[]{:S(2)}) copy-start(s32[2]{0:T(128)} %constant.65) | copy-start | bytes 28
  7.9 30.5 %copy-start.7 = (s32[2]{0:T(128)S(1)}, s32[2]{0:T(128)}, u32[]{:S(2)}) copy-start(s32[2]{0:T(128)} %constant.68) | copy-start | bytes 28
  33.6 17.3 %all-to-all-start.1 = ((bf16[8,32,1600]{2,1,0:T(8,128)(2,1)}), bf16[8,32,1600]{2,1,0:T(8,128)(2,1)S(1)}, u32[]{:S(2)}, u32[]{:S(2)}) async-start(bf16[8,32,1600]{2,1,0:T(8,128)(2,1)} %broadcast_in_dim.57), calls=%async_computation.1 | async-start | bytes 1703936 | tf_op jit(solution)/shard_map/all_to_all | solution.py:22
  56.7 35.0 %copy-start.3 = (f32[2,2048]{1,0:T(2,128)S(1)}, f32[2,2048]{1,0:T(2,128)}, u32[]{:S(2)}) copy-start(f32[2,2048]{1,0:T(2,128)} %param.12) | copy-start | bytes 49156
  56.7 35.0 %copy-start.4 = (f32[2,2048]{1,0:T(2,128)S(1)}, f32[2,2048]{1,0:T(2,128)}, u32[]{:S(2)}) copy-start(f32[2,2048]{1,0:T(2,128)} %param.11) | copy-start | bytes 49156
  56.7 35.0 %copy-start.5 = (s32[2,2048]{1,0:T(2,128)S(1)}, s32[2,2048]{1,0:T(2,128)}, u32[]{:S(2)}) copy-start(s32[2,2048]{1,0:T(2,128)} %param.13) | copy-start | bytes 49156
  136.5 22.7 %copy-start.1 = (f32[51200]{0:T(1024)S(1)}, f32[51200]{0:T(1024)}, u32[]{:S(2)}) copy-start(f32[51200]{0:T(1024)} %param.8) | copy-start | bytes 614404
  137.2 22.0 %copy-start = (f32[1,51200]{1,0:T(1,128)S(1)}, f32[1,51200]{1,0:T(1,128)}, u32[]{:S(2)}) copy-start(f32[1,51200]{1,0:T(1,128)} %param.7) | copy-start | bytes 614404
  138.0 16.2 %all-to-all-start.3 = ((bf16[32,2,800]{2,1,0:T(2,128)(2,1)}), bf16[32,2,800]{2,1,0:T(2,128)(2,1)S(1)}, u32[]{:S(2)}, u32[]{:S(2)}) async-start(bf16[32,2,800]{2,1,0:T(2,128)(2,1)} %reshape.148), calls=%async_computation.3 | async-start | bytes 229376 | tf_op jit(solution)/shard_map/all_to_all | solution.py:107
where the time goes:
time: 201 us; the launch traced here: 200 us
  blocking collectives  77.2 us (38%)
  local copies, waits for them, and re-layouts  40.4 us (20%)
  other arithmetic  40 us (20%)
  waiting for transfers between devices  21.7 us (11%)
  starting transfers between devices  10.2 us (5%)
  matrix products  7.25 us (4%)
  between operations  3.58 us (2%)
    psum x5, blocking collectives, by_axis(): value = lax.psum(value, axis)  38 us
    gather x3, local copies, waits for them, and re-layouts, per_device(): modelled = jnp.take_along_axis(cells_flat, obs_index, axis=1)  34.9 us
    unnamed x10, other arithmetic  28.7 us
    all_to_all x1, blocking collectives, per_device(): lax.all_to_all(member_field, SPACE, split_axis=1, concat_axis=0, tiled=True)  23.1 us
    all_to_all x1, blocking collectives, sent_and_summed(): lax.all_to_all(tiles, axis, split_axis=0, concat_axis=0, tiled=True)  16.1 us
    all_to_all x1, waiting for transfers between devices, from_everyone(): return lax.all_to_all(copies, axis, split_axis=0, concat_axis=0, tiled=True)  12.5 us
    all_to_all x1, waiting for transfers between devices, per_device(): lax.all_to_all(summed_rows.astype(jnp.bfloat16), SPACE, split_axis=0, con...  9.22 us
    all_to_all x1, starting transfers between devices, per_device(): lax.all_to_all(summed_rows.astype(jnp.bfloat16), SPACE, split_axis=0, con...  5.64 us
  transfers between devices with their start and end apart: 2, of which 2 were waited for; matrix products, arithmetic and copies ran while one was open for 0% of the time, Pallas kernels for 0%

commit v1 on v0

--- a/solution.py
+++ b/solution.py
@@ -40,7 +40,7 @@
 
 def by_axis(value, axes):
     for axis in axes:
-        value = lax.psum(value, axis)
+        value = jnp.sum(lax.all_gather(value, axis), axis=0)
     return value
 
 

time: 201 us -> 230 us (1.14)
  local copies, waits for them, and re-layouts: 40.4 us -> 63.7 us
  other arithmetic: 40 us -> 49.4 us
  blocking collectives: 77.2 us -> 74 us
    psum x5 -> x0, blocking collectives: 38 us -> none  [by_axis(): value = lax.psum(value, axis)]
    unnamed x0 -> x5, blocking collectives: none -> 34.7 us
    unnamed x26 -> x71, local copies, waits for them, and re-layouts: 2.63 us -> 25.9 us
    reduce_sum x0 -> x15, other arithmetic: none -> 9.33 us  [by_axis(): value = jnp.sum(lax.all_gather(value, axis), axis=0)]
  transfers between devices with their start and end apart: 2 -> 2, of which waited for: 2 -> 2; matrix products, arithmetic and copies ran while one was open for 0% -> 1% of each run, Pallas kernels for 0% -> 0%
where the time goes in v1:
time: 230 us; the launch traced here: 229 us
  blocking collectives  74 us (32%)
  local copies, waits for them, and re-layouts  63.7 us (28%)
  other arithmetic  49.4 us (21%)
  waiting for transfers between devices  19.7 us (9%)
  starting transfers between devices  10.2 us (4%)
  matrix products  7.25 us (3%)
  between operations  4.84 us (2%)
    gather x3, local copies, waits for them, and re-layouts, per_device(): modelled = jnp.take_along_axis(cells_flat, obs_index, axis=1)  34.9 us
    unnamed x5, blocking collectives  34.7 us
    unnamed x10, other arithmetic  28.7 us
    unnamed x71, local copies, waits for them, and re-layouts  25.9 us
    all_to_all x1, blocking collectives, per_device(): lax.all_to_all(member_field, SPACE, split_axis=1, concat_axis=0, tiled=True)  23.1 us
    all_to_all x1, blocking collectives, sent_and_summed(): lax.all_to_all(tiles, axis, split_axis=0, concat_axis=0, tiled=True)  16.1 us
    all_to_all x1, waiting for transfers between devices, from_everyone(): return lax.all_to_all(copies, axis, split_axis=0, concat_axis=0, tiled=True)  12.5 us
    reduce_sum x15, other arithmetic, by_axis(): value = jnp.sum(lax.all_gather(value, axis), axis=0)  9.33 us
  transfers between devices with their start and end apart: 2, of which 2 were waited for; matrix products, arithmetic and copies ran while one was open for 1% of the time, Pallas kernels for 0%

profile of v1, /device:TPU:1, one launch (start us, length us, event | category | flops | bytes accessed | tf_op | source)
XLA Modules:
  0.0 229.1 jit_solution(168027108157342685)
XLA Ops:
  0.7 2.4 %multiply_reduce_fusion.4 = (f32[]{:T(128)}, f32[51200]{0:T(1024)S(1)}) fusion(f32[1,51200]{1,0:T(1,128)} %param.7, f32[1,51200]{1,0:T(1,128)} %bitcast.77), kind=kLoop, calls=%fused_computation.22 | loop fusion | flops 153599 | bytes 614404 | tf_op jit(solution)/shard_map/reduce_sum | solution.py:95
  3.2 2.6 %convolution_bitcast_fusion.1 = f32[320,160]{0,1:T(8,128)S(1)} fusion(f32[320,160]{1,0:T(8,128)S(1)} %reshape.104, f32[320]{0:T(512)S(1)} %add_multiply_fusion, pred[320]{0:T(512)(128)(4,1)S(1)} %iota_compare_fusion), kind=kOutput, calls=%fused_computation.5 | convolution fusion | flops 197120000 | bytes 411200 | tf_op jit(solution)/shard_map/kn,mkl->mnl/dot_general | solution.py:58
  9.3 23.1 %all_to_all.36 = bf16[32,2,800]{2,1,0:T(2,128)(2,1)S(1)} all-to-all(bf16[32,2,800]{2,1,0:T(2,128)(2,1)S(1)} %reshape.221), channel_id=1, replica_groups=mesh['tm_0'=2,'tm_1'=4,'space_0'=4,'space_1'=4,'space_2'=2] {'space_0','..., dimensions={0} | all-to-all | bytes 204800 | tf_op jit(solution)/shard_map/all_to_all | solution.py:82
  33.6 4.5 %all-to-all-start.1 = ((bf16[8,32,1600]{2,1,0:T(8,128)(2,1)}), bf16[8,32,1600]{2,1,0:T(8,128)(2,1)S(1)}, u32[]{:S(2)}, u32[]{:S(2)}) async-start(bf16[8,32,1600]{2,1,0:T(8,128)(2,1)} %broadcast_in_dim.57), calls=%async_computation.1 | async-start | bytes 1703936 | tf_op jit(solution)/shard_map/all_to_all | solution.py:22
  38.5 12.5 %all-to-all-done.1 = bf16[8,32,1600]{2,1,0:T(8,128)(2,1)S(1)} async-done(((bf16[8,32,1600]{2,1,0:T(8,128)(2,1)}), bf16[8,32,1600]{2,1,0:T(8,128)(2,1)S(1)}, u32[]{:S(2)}, u32[]{:S(2)}) %all-to-all-start.1) | async-done | bytes 819232 | tf_op jit(solution)/shard_map/all_to_all | solution.py:22
  51.9 4.7 %multiply_reduce_fusion.1 = f32[1600,2,4]{0,2,1:T(4,128)S(1)} fusion(f32[1600,256]{1,0:T(8,128)S(1)} %copy.34, bf16[2,256,4,1600]{1,3,2,0:T(8,128)(2,1)} %param.9), kind=kLoop, calls=%fused_computation.3 | loop fusion | flops 9817600 | bytes 8243200 | tf_op jit(solution)/shard_map/dzab,zb->dab/dot_general | solution.py:84
  56.7 34.9 %gather_fusion = f32[4096]{0:T(1024)S(1)} fusion(f32[2,6400]{1,0:T(2,128)S(1)} %reshape.107, s32[4096]{0:T(1024)S(1)} %bitcast.73), kind=kCustom, calls=%fused_computation | custom fusion | bytes 65536 | tf_op jit(solution)/shard_map/jit(take_along_axis)/gather | solution.py:91
  92.5 22.1 %scatter_custom_fusion = f32[12800]{0:T(1024)S(1)} fusion(s32[4096]{0:T(1024)S(1)} %bitcast.82, f32[4096]{0:T(1024)S(1)} %bitcast.83, f32[]{:T(128)} %constant.18.clone.1), kind=kCustom, calls=%fused_computation.44 | custom fusion | flops 4096 | bytes 51204
  114.7 4.8 %multiply_reduce_fusion = bf16[1600,256]{1,0:T(8,128)(2,1)S(1)} fusion(f32[1600,2,4]{0,2,1:T(4,128)S(1)} %bitcast_convert_fusion.1, bf16[2,256,4,1600]{1,3,2,0:T(8,128)(2,1)} %param.9), kind=kLoop, calls=%fused_computation.2 | loop fusion | flops 9420800 | bytes 7424000
  120.2 16.1 %all_to_all.37 = bf16[8,32,1600]{2,1,0:T(8,128)(2,1)S(1)} all-to-all(bf16[8,32,1600]{2,1,0:T(8,128)(2,1)S(1)} %bitcast.74), channel_id=1, replica_groups=mesh['tm_0'=2,'tm_1'=4,'space_0'=4,'space_1'=4,'space_2'=2] {'tm_0','tm_1'}, dimensions={0} | all-to-all | bytes 1638400 | tf_op jit(solution)/shard_map/all_to_all | solution.py:37
  138.1 5.6 %all-to-all-start.3 = ((bf16[32,2,800]{2,1,0:T(2,128)(2,1)}), bf16[32,2,800]{2,1,0:T(2,128)(2,1)S(1)}, u32[]{:S(2)}, u32[]{:S(2)}) async-start(bf16[32,2,800]{2,1,0:T(2,128)(2,1)} %reshape.223), calls=%async_computation.3 | async-start | bytes 229376 | tf_op jit(solution)/shard_map/all_to_all | solution.py:107
  145.6 1.4 dynamic-update-slice.5
  147.0 7.3 %all-to-all-done.3 = bf16[32,2,800]{2,1,0:T(2,128)(2,1)S(1)} async-done(((bf16[32,2,800]{2,1,0:T(2,128)(2,1)}), bf16[32,2,800]{2,1,0:T(2,128)(2,1)S(1)}, u32[]{:S(2)}, u32[]{:S(2)}) %all-to-all-start.3) | async-done | bytes 102432 | tf_op jit(solution)/shard_map/all_to_all | solution.py:107
  155.3 2.3 %convolution_bitcast_fusion = f32[320,160]{0,1:T(8,128)S(1)} fusion(bf16[320,160]{1,0:T(8,128)(2,1)S(1)} %reshape.111, f32[320]{0:T(512)S(1)} %add_multiply_fusion, pred[320]{0:T(512)(128)(4,1)S(1)} %iota_compare_fusion), kind=kOutput, calls=%fused_computation.4 | convolution fusion | flops 197120000 | bytes 308800 | tf_op jit(solution)/shard_map/kn,mnp->mkp/dot_general | solution.py:65
  160.3 1.3 dynamic-update-slice.10
  162.2 3.8 %all-reduce.19 = (f32[2]{0:T(128)S(1)}, f32[2]{0:T(128)S(1)}, f32[2]{0:T(128)S(1)}) all-reduce(f32[2]{0:T(128)S(1)} %dynamic-update-slice, f32[2]{0:T(128)S(1)} %dynamic-update-slice.5, f32[2]{0:T(128)S(1)} %dynamic-update-slice.10), channel_id=1, replica_groups=mesh['tm_0'=2,'tm_1'=4,'space_0'=4,'space_1'=4,'space_2'=2] {'tm_0'}, use_global_device_ids=true, to_apply=%add | all-reduce | flops 6 | bytes 48
  167.3 1.4 dynamic-update-slice.11
  168.7 1.4 dynamic-update-slice.6
  170.7 1.4 dynamic-update-slice.1
  172.7 7.1 %all-reduce.17 = (f32[4]{0:T(128)S(1)}, f32[4]{0:T(128)S(1)}, f32[4]{0:T(128)S(1)}) all-reduce(f32[4]{0:T(128)S(1)} %dynamic-update-slice.1, f32[4]{0:T(128)S(1)} %dynamic-update-slice.6, f32[4]{0:T(128)S(1)} %dynamic-update-slice.11), channel_id=1, replica_groups=mesh['tm_0'=2,'tm_1'=4,'space_0'=4,'space_1'=4,'space_2'=2] {'tm_1'}, use_global_device_ids=true, to_apply=%add.1 | all-reduce | flops 12 | bytes 96
  181.1 1.4 dynamic-update-slice.12
  182.5 1.4 dynamic-update-slice.7
  184.5 1.4 dynamic-update-slice.2
  186.5 7.7 %all-reduce.16 = (f32[4]{0:T(128)S(1)}, f32[4]{0:T(128)S(1)}, f32[4]{0:T(128)S(1)}) all-reduce(f32[4]{0:T(128)S(1)} %dynamic-update-slice.2, f32[4]{0:T(128)S(1)} %dynamic-update-slice.7, f32[4]{0:T(128)S(1)} %dynamic-update-slice.12), channel_id=1, replica_groups=mesh['tm_0'=2,'tm_1'=4,'space_0'=4,'space_1'=4,'space_2'=2] {'space_0'}, use_global_device_ids=true, to_apply=%add.2 | all-reduce | flops 12 | bytes 96
  195.5 1.4 dynamic-update-slice.13
  196.9 1.4 dynamic-update-slice.8
  198.9 1.4 dynamic-update-slice.3
  200.9 6.3 %all-reduce.15 = (f32[4]{0:T(128)S(1)}, f32[4]{0:T(128)S(1)}, f32[4]{0:T(128)S(1)}) all-reduce(f32[4]{0:T(128)S(1)} %dynamic-update-slice.3, f32[4]{0:T(128)S(1)} %dynamic-update-slice.8, f32[4]{0:T(128)S(1)} %dynamic-update-slice.13), channel_id=1, replica_groups=mesh['tm_0'=2,'tm_1'=4,'space_0'=4,'space_1'=4,'space_2'=2] {'space_1'}, use_global_device_ids=true, to_apply=%add.3 | all-reduce | flops 12 | bytes 96
  208.5 1.4 dynamic-update-slice.14
  209.9 1.4 dynamic-update-slice.9
  211.9 1.4 dynamic-update-slice.4
  213.3 9.9 %all-reduce.18 = (f32[2]{0:T(128)S(1)}, f32[2]{0:T(128)S(1)}, f32[2]{0:T(128)S(1)}) all-reduce(f32[2]{0:T(128)S(1)} %dynamic-update-slice.4, f32[2]{0:T(128)S(1)} %dynamic-update-slice.9, f32[2]{0:T(128)S(1)} %dynamic-update-slice.14), channel_id=1, replica_groups=mesh['tm_0'=2,'tm_1'=4,'space_0'=4,'space_1'=4,'space_2'=2] {'space_2'}, use_global_device_ids=true, to_apply=%add.4 | all-reduce | flops 6 | bytes 48
  (106 shorter events, 26.9 us)
Async XLA Ops:
  7.3 30.8 %copy-start.2 = (s32[2,2048]{1,0:T(2,128)S(1)}, s32[2,2048]{1,0:T(2,128)}, u32[]{:S(2)}) copy-start(s32[2,2048]{1,0:T(2,128)} %param.10) | copy-start | bytes 49156
  7.9 30.4 %copy-start.6 = (s32[2]{0:T(128)S(1)}, s32[2]{0:T(128)}, u32[]{:S(2)}) copy-start(s32[2]{0:T(128)} %constant.65) | copy-start | bytes 28
  7.9 30.5 %copy-start.7 = (s32[2]{0:T(128)S(1)}, s32[2]{0:T(128)}, u32[]{:S(2)}) copy-start(s32[2]{0:T(128)} %constant.68) | copy-start | bytes 28
  33.6 17.3 %all-to-all-start.1 = ((bf16[8,32,1600]{2,1,0:T(8,128)(2,1)}), bf16[8,32,1600]{2,1,0:T(8,128)(2,1)S(1)}, u32[]{:S(2)}, u32[]{:S(2)}) async-start(bf16[8,32,1600]{2,1,0:T(8,128)(2,1)} %broadcast_in_dim.57), calls=%async_computation.1 | async-start | bytes 1703936 | tf_op jit(solution)/shard_map/all_to_all | solution.py:22
  56.7 35.0 %copy-start.3 = (f32[2,2048]{1,0:T(2,128)S(1)}, f32[2,2048]{1,0:T(2,128)}, u32[]{:S(2)}) copy-start(f32[2,2048]{1,0:T(2,128)} %param.12) | copy-start | bytes 49156
  56.7 35.0 %copy-start.4 = (f32[2,2048]{1,0:T(2,128)S(1)}, f32[2,2048]{1,0:T(2,128)}, u32[]{:S(2)}) copy-start(f32[2,2048]{1,0:T(2,128)} %param.11) | copy-start | bytes 49156
  56.7 35.0 %copy-start.5 = (s32[2,2048]{1,0:T(2,128)S(1)}, s32[2,2048]{1,0:T(2,128)}, u32[]{:S(2)}) copy-start(s32[2,2048]{1,0:T(2,128)} %param.13) | copy-start | bytes 49156
  119.5 24.2 %copy-start.12 = (u32[256]{0:T(256)S(1)}, u32[256]{0:T(256)}, u32[]{:S(2)}) copy-start(u32[256]{0:T(256)} %constant.88) | copy-start | bytes 3076
  136.5 22.7 %copy-start.1 = (f32[51200]{0:T(1024)S(1)}, f32[51200]{0:T(1024)}, u32[]{:S(2)}) copy-start(f32[51200]{0:T(1024)} %param.8) | copy-start | bytes 614404
  137.2 22.0 %copy-start = (f32[1,51200]{1,0:T(1,128)S(1)}, f32[1,51200]{1,0:T(1,128)}, u32[]{:S(2)}) copy-start(f32[1,51200]{1,0:T(1,128)} %param.7) | copy-start | bytes 614404
  138.1 16.2 %all-to-all-start.3 = ((bf16[32,2,800]{2,1,0:T(2,128)(2,1)}), bf16[32,2,800]{2,1,0:T(2,128)(2,1)S(1)}, u32[]{:S(2)}, u32[]{:S(2)}) async-start(bf16[32,2,800]{2,1,0:T(2,128)(2,1)} %reshape.223), calls=%async_computation.3 | async-start | bytes 229376 | tf_op jit(solution)/shard_map/all_to_all | solution.py:107
  147.0 14.6 %copy-start.11 = (u32[256]{0:T(256)S(1)}, u32[256]{0:T(256)}, u32[]{:S(2)}) copy-start(u32[256]{0:T(256)} %constant.93) | copy-start | bytes 3076
  147.0 25.1 %copy-start.10 = (u32[256]{0:T(256)S(1)}, u32[256]{0:T(256)}, u32[]{:S(2)}) copy-start(u32[256]{0:T(256)} %constant.98) | copy-start | bytes 3076
  154.4 31.5 %copy-start.9 = (u32[256]{0:T(256)S(1)}, u32[256]{0:T(256)}, u32[]{:S(2)}) copy-start(u32[256]{0:T(256)} %constant.103) | copy-start | bytes 3076
  154.5 45.9 %copy-start.8 = (u32[256]{0:T(256)S(1)}, u32[256]{0:T(256)}, u32[]{:S(2)}) copy-start(u32[256]{0:T(256)} %constant.108) | copy-start | bytes 3076
